TPU v7x, 256 devices: a whole 4x4x8 slice. The times are simulated.
256 devices in a mesh: strip: 64 (over x, z, core), chan: 4 (over y).
Axes of the slice: x: 4, y: 4, z: 8, core: 2. Of those that a mesh axis runs over, the one named last changes fastest.
Arguments:
- section_input: bfloat16 [48, 8192, 256], P(None, 'strip'), may hold values from -6 to 6
- conv_weight: bfloat16 [3, 3, 256, 256], replicated, may hold values from -0.125 to 0.125
- conv_bias: float32 [256], replicated, may hold values from -3 to 3
- deep_weight: bfloat16 [3, 3, 256, 512], P(None, None, None, 'chan'), may hold values from -0.125 to 0.125
- deep_bias: float32 [512], P('chan'), may hold values from -3 to 3
- labels: int32 [24, 4096], P(None, 'strip'), may hold values from 0 to 32, as said below
- slot_ids: int32 [2048], P('strip'), may hold values from 0 to 4095, as said below
- embed_grad: float32 [4096, 512], P('strip', 'chan'), may hold values from -0.8 to 0.8
Outputs:
- embeddings: float32 [4096, 512], P('strip', 'chan')
- weight_grad: float32 [3, 3, 256, 512], P(None, None, None, 'chan')
- bias_grad: float32 [512], P('chan')
Inputs may be any that keep to these rules, and one draw needn't show every extreme that they name: `labels`: the value 32 marks background; any other value v names entry v of the list of the strip that holds the pixel. `slot_ids`: A value s names slot s % 64 of owner s // 64 (an index of strip). The slots within one strip's list differ; a slot stands in the lists of at most two strips, which are neighbours (a crack across a strip border). Every owner holds at most 64 components and some owner holds exactly 64.
All inputs are finite; a program needn't handle non-finite values.
Results may differ from a plain program's by a relative error of at most 0.0035.
Values may be sent and summed in bfloat16 or wider, within the bound.
A program may use at most 64 MiB of HBM per device.

v0:
```python
import jax
import jax.numpy as jnp
from jax import lax
from jax.sharding import PartitionSpec as P


def with_halo(cells, sides, width):
    for axis, dim in sides:
        count = lax.axis_size(axis)
        ends = count - 1
        head = lax.slice_in_dim(cells, 0, width, axis=dim)
        tail = lax.slice_in_dim(cells, cells.shape[dim] - width, cells.shape[dim], axis=dim)
        cells = jnp.concatenate(
            [
                lax.ppermute(tail, axis, [(i, (i + 1) % count) for i in range(ends)]),
                cells,
                lax.ppermute(head, axis, [((i + 1) % count, i) for i in range(ends)]),
            ],
            axis=dim,
        )
    return cells


def swish(value):
    return value * jax.nn.sigmoid(value)


def swish_slope(value):
    sigma = jax.nn.sigmoid(value)
    return sigma * (1.0 + value * (1.0 - sigma))


def convolve(padded, weight, row_count, col_count):
    channels = padded.shape[-1]
    running = None
    for shift_row in range(3):
        for shift_col in range(3):
            window = padded[
                shift_row : shift_row + row_count, shift_col : shift_col + col_count
            ].reshape(row_count * col_count, channels)
            partial_term = jnp.dot(
                window, weight[shift_row, shift_col], preferred_element_type=jnp.float32
            )
            running = partial_term if running is None else running + partial_term
    return running.reshape(row_count, col_count, weight.shape[-1])


def pool_pairs(hidden):
    row_count, col_count, channels = hidden.shape
    return (
        hidden.reshape(row_count // 2, 2, col_count // 2, 2, channels)
        .mean(axis=(1, 3))
        .astype(jnp.bfloat16)
    )


def body(
    section_input, conv_weight, conv_bias, deep_weight, deep_bias, labels, slot_ids, embed_grad
):
    chan_count = lax.axis_size("chan")
    chan_pos = lax.axis_index("chan")
    strip_count = lax.axis_size("strip")
    strip_pos = lax.axis_index("strip")
    row_total, col_local, channels = section_input.shape
    row_part = row_total // chan_count
    half_cols = col_local // 2
    padded_rows = jnp.pad(section_input, ((1, 1), (0, 0), (0, 0)))
    own_rows = lax.dynamic_slice_in_dim(padded_rows, chan_pos * row_part, row_part + 2, 0)
    extended = with_halo(own_rows, (("strip", 1),), 3)
    hidden = swish(convolve(extended, conv_weight, row_part, col_local + 4) + conv_bias)
    pooled = pool_pairs(hidden)
    column = jnp.arange(half_cols + 2)
    outside = (column == 0) & (strip_pos == 0) | (column == half_cols + 1) & (
        strip_pos == strip_count - 1
    )
    pooled = jnp.where(outside[None, :, None], jnp.zeros_like(pooled), pooled)
    gathered = lax.all_gather(pooled, "chan", axis=0, tiled=True)
    padded_deep = jnp.pad(gathered, ((1, 1), (0, 0), (0, 0)))
    half_rows = gathered.shape[0]
    deep_pre = convolve(padded_deep, deep_weight, half_rows, half_cols) + deep_bias
    width_deep = deep_weight.shape[-1]
    features = swish(deep_pre).astype(jnp.bfloat16).reshape(-1, width_deep)
    flat_labels = labels.reshape(-1)
    list_len = slot_ids.shape[0]
    member = flat_labels[None, :] == jnp.arange(list_len, dtype=jnp.int32)[:, None]
    part_sums = jnp.dot(member.astype(jnp.bfloat16), features, preferred_element_type=jnp.float32)
    part_counts = jnp.sum(member.astype(jnp.float32), axis=1)
    owned = embed_grad.shape[0]
    dense_sums = (
        jnp.zeros((owned * strip_count, width_deep), jnp.float32).at[slot_ids].set(part_sums)
    )
    dense_counts = jnp.zeros((owned * strip_count,), jnp.float32).at[slot_ids].set(part_counts)
    slot_sums, slot_counts = (
        lax.psum_scatter(dense_sums, "strip", scatter_dimension=0, tiled=True),
        lax.psum_scatter(dense_counts, "strip", scatter_dimension=0, tiled=True),
    )
    divisor = jnp.maximum(slot_counts, 1.0)[:, None]
    embeddings = slot_sums / divisor
    every_grad = lax.all_gather(embed_grad / divisor, "strip", axis=0, tiled=True)
    entry_grad = every_grad[slot_ids]
    pixel_grad = lax.dot_general(
        member.astype(jnp.float32),
        entry_grad,
        (((0,), (0,)), ((), ())),
        precision=lax.Precision.HIGHEST,
        preferred_element_type=jnp.float32,
    )
    deep_grad = (pixel_grad * swish_slope(deep_pre.reshape(-1, width_deep))).astype(jnp.bfloat16)
    pieces = []
    for shift_row in range(3):
        for shift_col in range(3):
            window = padded_deep[
                shift_row : shift_row + half_rows, shift_col : shift_col + half_cols
            ].reshape(-1, channels)
            pieces.append(
                lax.dot_general(
                    window, deep_grad, (((0,), (0,)), ((), ())), preferred_element_type=jnp.float32
                )
            )
    local_weight = jnp.stack(pieces).reshape(3, 3, channels, width_deep)
    local_bias = jnp.sum(deep_grad.astype(jnp.float32), axis=0)
    weight_grad, bias_grad = lax.psum((local_weight, local_bias), "strip")
    return (embeddings, weight_grad, bias_grad)


def solution(mesh):
    placed = (
        P(None, "strip", None),
        P(),
        P(),
        P(None, None, None, "chan"),
        P("chan"),
        P(None, "strip"),
        P("strip"),
        P("strip", "chan"),
    )
    return jax.shard_map(
        body,
        mesh=mesh,
        in_specs=placed,
        out_specs=(P("strip", "chan"), P(None, None, None, "chan"), P("chan")),
        check_vma=False,
    )
```

profile of v0, /device:TPU:8, one launch (start us, length us, event | category | flops | bytes accessed | tf_op | source)
XLA Modules:
  0.0 597.8 jit_solution(9862695185246819074)
XLA Ops:
  7.2 1.0 pad_dynamic-slice_fusion.1
  8.3 1.3 collective-permute-start.1
  9.6 3.0 collective-permute-start
  12.6 1.0 pad_dynamic-slice_fusion.2
  13.8 1.6 pad_maximum_fusion
  15.4 2.6 fusion.59
  17.9 2.1 reshape.94
  20.0 2.0 reshape.93
  22.0 2.1 reshape.95
  24.1 2.1 reshape.96
  26.1 2.1 reshape.97
  28.2 1.0 reshape.98
  29.2 1.0 reshape.99
  30.4 1.1 reshape.101
  31.5 1.4 fusion.23
  34.6 0.8 copy-done.16
  36.9 0.8 copy-done.14
  40.7 1.0 reshape.102
  41.7 2.7 fusion.2
  44.5 15.0 %all_gather.6 = bf16[24,66,256]{2,1,0:T(8,128)(2,1)S(1)} all-gather(bf16[6,66,256]{2,1,0:T(8,128)(2,1)S(1)} %fusion.15), channel_id=1, replica_groups=mesh['strip'=64,'chan'=4] {'chan'}, dimensions={0}, use_global_device_ids=true | all-gather | bytes 1013760 | tf_op jit(solution)/shard_map/all_gather | solution.py:77
  59.5 1.4 pad_slice_fusion
  65.2 0.9 copy-done.21
  66.5 2.1 scatter_custom_fusion
  70.7 251.7 %all-reduce.2 = f32[4096]{0:T(1024)S(1)} all-reduce(f32[4096]{0:T(1024)S(1)} %scatter_custom_fusion.1), channel_id=3, replica_groups=mesh['strip'=64,'chan'=4] {'strip'}, use_global_device_ids=true, to_apply=%region_5.6.clone | all-reduce | flops 4096 | bytes 32768
  322.5 1.5 broadcast_divide_fusion
  324.1 70.7 %all-gather.2.cloned.1.call-done = f32[4096,128]{1,0:T(8,128)} async-done(((f32[64,128]{1,0:T(8,128)}), f32[4096,128]{1,0:T(8,128)}) %all-gather.2.cloned.1.call-update) | async-done | bytes 2097168 | tf_op jit(solution)/shard_map/all_gather | solution.py:99
  394.8 2.2 gather_fusion
  397.0 2.1 convert_reduce_fusion
  403.5 1.0 copy-done.19
  404.5 127.1 %psum.15 = f32[128]{0:T(128)} all-reduce(f32[128]{0:T(128)S(1)} %get-tuple-element.25), channel_id=1, replica_groups=mesh['strip'=64,'chan'=4] {'strip'}, use_global_device_ids=true, to_apply=%region_8.9 | all-reduce | flops 128 | bytes 1024 | tf_op jit(solution)/shard_map/psum | solution.py:122
  531.6 57.3 %all-reduce.5.cloned.1.call-done = f32[3,3,256,128]{3,2,1,0:T(8,128)} async-done(((f32[3,3,256,128]{3,2,1,0:T(8,128)}), f32[3,3,256,128]{3,2,1,0:T(8,128)}) %all-reduce.5.cloned.1.call-update) | async-done | bytes 1179664 | tf_op jit(solution)/shard_map/psum | solution.py:122
  588.9 2.4 copy.20
  (100 shorter events, 17.1 us)
Async XLA Ops:
  7.2 5.5 copy-start
  7.2 315.3 %reduce-scatter.2.cloned.1.call-start = ((), (), s32[]{:S(2)}) async-start(), calls=%async_computation.1 | async-start | bytes 2129920 | tf_op jit(solution)/shard_map/reduce_scatter | solution.py:94
  8.3 5.5 collective-permute-start.1
  9.6 4.1 copy-start.27
  9.6 4.1 copy-start.24
  9.6 4.2 collective-permute-start
  30.3 1.2 copy-start.11
  31.5 1.4 copy-start.18
  31.5 1.6 copy-start.20
  33.1 1.1 copy-start.17
  34.2 1.1 copy-start.16
  35.4 1.1 copy-start.15
  36.5 1.1 copy-start.14
  37.6 1.1 copy-start.13
  39.2 1.1 copy-start.12
  40.7 1.0 copy-start.25
  59.5 1.5 copy-start.22
  60.9 1.1 copy-start.9
  60.9 1.4 copy-start.5
  60.9 1.7 copy-start.3
  61.0 2.1 copy-start.1
  65.2 0.9 copy-start.21
  66.4 3.0 copy-start.28
  66.4 256.1 %copy-start.23 = (f32[64,128]{1,0:T(8,128)S(1)}, f32[64,128]{1,0:T(8,128)}, u32[]{:S(2)}) copy-start(f32[64,128]{1,0:T(8,128)} %param.15) | copy-start | bytes 98308
  68.6 326.2 %all-gather.2.cloned.1.call-start = ((), (), s32[]{:S(2)}) async-start(), calls=%async_computation.2 | async-start | bytes 2129920 | tf_op jit(solution)/shard_map/all_gather | solution.py:99
  324.0 264.9 %all-reduce.5.cloned.1.call-start = ((), (), s32[]{:S(2)}) async-start(), calls=%async_computation.3 | async-start | bytes 2359296 | tf_op jit(solution)/shard_map/psum | solution.py:122
  396.9 2.1 copy-start.10
  397.0 2.5 copy-start.8
  399.1 1.1 copy-start.6
  399.5 1.2 copy-start.4
  400.2 1.2 copy-start.2
  403.5 1.0 copy-start.19
  (2 other events, 1.5 us)
Sparse Core Ops, SparseCore 0:
  68.7 145.5 reduce-scatter.1
  324.1 70.6 all-gather.1
  404.6 184.2 all-reduce.4
where the time goes:
time: 599 us; the launch traced here: 598 us
  blocking collectives  394 us (66%)
  waiting for transfers between devices  128 us (21%)
  local copies, waits for them, and re-layouts  36.6 us (6%)
  between operations  14.9 us (2%)
  matrix products  13.8 us (2%)
  other arithmetic  6.09 us (1%)
    unnamed x1, blocking collectives  252 us
    psum x1, blocking collectives, body(): weight_grad, bias_grad = lax.psum((local_weight, local_bias), 'strip')  127 us
    all_gather x1, waiting for transfers between devices, body(): lax.all_gather(embed_grad / divisor, 'strip', axis=0, tiled=True)  70.7 us
    psum x1, waiting for transfers between devices, body(): weight_grad, bias_grad = lax.psum((local_weight, local_bias), 'strip')  57.3 us
    all_gather x1, blocking collectives, body(): gathered = lax.all_gather(pooled, 'chan', axis=0, tiled=True)  15 us
    reshape x9, local copies, waits for them, and re-layouts, convolve(): window = padded[shift_row:shift_row + row_count, shift_col:shift_col + co...  13.6 us
  transfers between devices with their start and end apart: 5, of which 2 were waited for; matrix products, arithmetic and copies ran while one was open for 0% of the time, Pallas kernels for 0%

commit v1 on v0

--- a/solution.py
+++ b/solution.py
@@ -96,7 +96,13 @@
     )
     divisor = jnp.maximum(slot_counts, 1.0)[:, None]
     embeddings = slot_sums / divisor
-    every_grad = lax.all_gather(embed_grad / divisor, "strip", axis=0, tiled=True)
+    z = embed_grad / divisor
+    every_grad = jnp.concatenate(
+        lax.all_to_all(
+            jnp.stack([z for _ in range(lax.axis_size("strip"))], axis=0), "strip", 0, 0
+        ),
+        0,
+    )
     entry_grad = every_grad[slot_ids]
     pixel_grad = lax.dot_general(
         member.astype(jnp.float32),

time: 599 us -> 585 us (0.977)
  waiting for transfers between devices: 128 us -> 109 us
    all_gather x1 -> x0, waiting for transfers between devices: 70.7 us -> none  [body(): lax.all_gather(embed_grad / divisor, 'strip', axis=0, tiled=True)]
    all_to_all x0 -> x1, waiting for transfers between devices: none -> 51 us  [body(): lax.all_to_all(jnp.stack([z for _ in range(lax.axis_size('strip'))], axis...]
where the time goes in v1:
time: 585 us; the launch traced here: 584 us
  blocking collectives  392 us (67%)
  waiting for transfers between devices  109 us (19%)
  local copies, waits for them, and re-layouts  38.3 us (7%)
  between operations  15.2 us (3%)
  matrix products  13.8 us (2%)
  starting transfers between devices  9.97 us (2%)
  other arithmetic  6.08 us (1%)
    unnamed x1, blocking collectives  252 us
    psum x1, blocking collectives, body(): weight_grad, bias_grad = lax.psum((local_weight, local_bias), 'strip')  125 us
    psum x1, waiting for transfers between devices, body(): weight_grad, bias_grad = lax.psum((local_weight, local_bias), 'strip')  57.6 us
    all_to_all x1, waiting for transfers between devices, body(): lax.all_to_all(jnp.stack([z for _ in range(lax.axis_size('strip'))], axis...  51 us
    all_gather x1, blocking collectives, body(): gathered = lax.all_gather(pooled, 'chan', axis=0, tiled=True)  15.1 us
    reshape x9, local copies, waits for them, and re-layouts, convolve(): window = padded[shift_row:shift_row + row_count, shift_col:shift_col + co...  13.6 us
  transfers between devices with their start and end apart: 5, of which 2 were waited for; matrix products, arithmetic and copies ran while one was open for 0% of the time, Pallas kernels for 0%

profile of v1, /device:TPU:8, one launch (start us, length us, event | category | flops | bytes accessed | tf_op | source)
XLA Modules:
  0.0 583.9 jit_solution(12276055326656072925)
XLA Ops:
  7.2 1.0 pad_dynamic-slice_fusion.1
  8.3 1.3 collective-permute-start.1
  9.6 3.0 collective-permute-start
  12.6 1.0 pad_dynamic-slice_fusion.2
  13.8 1.6 pad_maximum_fusion
  15.4 2.5 fusion.59
  17.9 2.1 reshape.99
  20.0 2.0 reshape.98
  22.0 2.1 reshape.100
  24.1 2.1 reshape.101
  26.2 2.0 reshape.102
  28.2 1.0 reshape.103
  29.2 1.0 reshape.104
  30.4 1.1 reshape.106
  31.5 1.4 fusion.23
  40.7 1.0 reshape.107
  41.7 2.7 fusion.2
  44.5 15.1 %all_gather.3 = bf16[24,66,256]{2,1,0:T(8,128)(2,1)S(1)} all-gather(bf16[6,66,256]{2,1,0:T(8,128)(2,1)S(1)} %fusion.15), channel_id=1, replica_groups=mesh['strip'=64,'chan'=4] {'chan'}, dimensions={0}, use_global_device_ids=true | all-gather | bytes 1013760 | tf_op jit(solution)/shard_map/all_gather | solution.py:77
  59.6 1.4 pad_slice_fusion
  65.3 0.9 copy-done.21
  66.6 2.1 scatter_custom_fusion
  70.8 251.7 %all-reduce.2 = f32[4096]{0:T(1024)S(1)} all-reduce(f32[4096]{0:T(1024)S(1)} %scatter_custom_fusion.1), channel_id=3, replica_groups=mesh['strip'=64,'chan'=4] {'strip'}, use_global_device_ids=true, to_apply=%region_5.6.clone | all-reduce | flops 4096 | bytes 32768
  322.6 1.5 broadcast_divide_fusion
  324.0 1.6 stack.22
  325.6 5.6 all-to-all-start
  331.2 51.0 %all-to-all-done = f32[64,64,128]{2,1,0:T(8,128)} async-done(((f32[64,64,128]{2,1,0:T(8,128)}), f32[64,64,128]{2,1,0:T(8,128)}, u32[]{:S(2)}, u32[]{:S(2)}) %all-to-all-start) | async-done | bytes 2097184 | tf_op jit(solution)/shard_map/all_to_all | solution.py:101
  382.2 2.2 gather_fusion
  384.4 2.1 convert_reduce_fusion
  390.9 1.0 copy-done.19
  391.9 125.2 %psum.15 = f32[128]{0:T(128)} all-reduce(f32[128]{0:T(128)S(1)} %get-tuple-element.25), channel_id=1, replica_groups=mesh['strip'=64,'chan'=4] {'strip'}, use_global_device_ids=true, to_apply=%region_8.9 | all-reduce | flops 128 | bytes 1024 | tf_op jit(solution)/shard_map/psum | solution.py:128
  517.1 57.6 %all-reduce.5.cloned.1.call-done = f32[3,3,256,128]{3,2,1,0:T(8,128)} async-done(((f32[3,3,256,128]{3,2,1,0:T(8,128)}), f32[3,3,256,128]{3,2,1,0:T(8,128)}) %all-reduce.5.cloned.1.call-update) | async-done | bytes 1179664 | tf_op jit(solution)/shard_map/psum | solution.py:128
  574.7 2.4 copy.20
  (100 shorter events, 18.6 us)
Async XLA Ops:
  7.2 5.5 copy-start
  7.2 315.4 %reduce-scatter.2.cloned.1.call-start = ((), (), s32[]{:S(2)}) async-start(), calls=%async_computation.2 | async-start | bytes 2129920 | tf_op jit(solution)/shard_map/reduce_scatter | solution.py:94
  8.3 5.5 collective-permute-start.1
  9.6 4.1 copy-start.27
  9.6 4.1 copy-start.24
  9.6 4.2 collective-permute-start
  30.3 1.2 copy-start.11
  31.5 1.4 copy-start.18
  31.5 1.6 copy-start.20
  33.1 1.1 copy-start.17
  34.2 1.1 copy-start.16
  35.4 1.1 copy-start.15
  36.5 1.1 copy-start.14
  37.7 1.1 copy-start.13
  39.2 1.1 copy-start.12
  40.7 1.0 copy-start.25
  59.6 1.5 copy-start.22
  61.0 1.1 copy-start.9
  61.0 1.4 copy-start.5
  61.0 1.8 copy-start.3
  61.0 2.2 copy-start.1
  65.3 0.9 copy-start.21
  66.5 3.0 copy-start.28
  66.6 256.0 %copy-start.23 = (f32[64,128]{1,0:T(8,128)S(1)}, f32[64,128]{1,0:T(8,128)}, u32[]{:S(2)}) copy-start(f32[64,128]{1,0:T(8,128)} %param.15) | copy-start | bytes 98308
  325.6 56.6 %all-to-all-start = ((f32[64,64,128]{2,1,0:T(8,128)}), f32[64,64,128]{2,1,0:T(8,128)}, u32[]{:S(2)}, u32[]{:S(2)}) async-start(f32[64,64,128]{2,1,0:T(8,128)} %stack.22), calls=%async_computation.1 | async-start | bytes 4194304 | tf_op jit(solution)/shard_map/all_to_all | solution.py:101
  331.2 243.6 %all-reduce.5.cloned.1.call-start = ((), (), s32[]{:S(2)}) async-start(), calls=%async_computation.3 | async-start | bytes 2359296 | tf_op jit(solution)/shard_map/psum | solution.py:128
  384.4 2.1 copy-start.10
  384.4 2.5 copy-start.8
  386.5 1.1 copy-start.6
  386.9 1.2 copy-start.4
  387.6 1.2 copy-start.2
  390.9 1.0 copy-start.19
  (2 other events, 1.6 us)
Sparse Core Ops, SparseCore 0:
  68.8 145.4 reduce-scatter.1
  392.0 182.6 all-reduce.4
